TPU v7x, 32 devices: a whole 2x2x4 slice. The times are simulated.
32 devices in a mesh: ent: 16 (over z, y, x), rep: 2 (over core).
Axes of the slice: x: 2, y: 2, z: 4, core: 2. Of those that a mesh axis runs over, the one named last changes fastest.
Arguments:
- head_ids: int32 [8192], P(('ent', 'rep')), may hold values from 0 to 32767, as said below
- rel_ids: int32 [8192], P(('ent', 'rep')), may hold values from 0 to 4095
- tail_ids: int32 [8192], P(('ent', 'rep')), may hold values from 0 to 32767, as said below
- neg_ids: int32 [256], P('ent'), may hold values from 0 to 32767, as said below
- slot_of: int32 [32768], replicated, may hold values from 0 to 32767, as said below
- relations: bfloat16 [4096, 400], replicated, may hold values from -3 to 3
- embeddings: float32 [32768, 400], P('ent'), may hold values from -1.75 to 1.75
- accumulator: float32 [32768], P('ent'), may hold values from 0.001 to 0.03
Outputs:
- new_embeddings: float32 [32768, 400], P('ent')
- new_accumulator: float32 [32768], P('ent')
Inputs may be any that keep to these rules, and one draw needn't show every extreme that they name: A permutation: every table row stores exactly one entity; the owner of entity e is slot_of[e] // 2048. `head_ids`: among the 512 endpoints (heads and tails together) of the edges of one device, at most 64 have any one owner; in every draw one owner has exactly 64 endpoints of every device. `tail_ids`: see head_ids: the bound counts heads and tails of one device together. `neg_ids`: entry j has owner j // 16.
All inputs are finite; a program needn't handle non-finite values.
Results may differ from a plain program's by a relative error of at most 0.0031.
Values may be sent and summed in bfloat16 or wider, within the bound.
No kernel may reach another device: no remote copies, remote signals or barrier semaphores. Data moves between devices by JAX's collectives and lax.ppermute only.
A program may use at most 128 MiB of HBM per device.

v0:
```python
import jax
import jax.numpy as jnp
from jax import lax
from jax.sharding import PartitionSpec as P

step_rate = 0.3


def split_parts(values):
    cut = values.shape[1] // 2
    return (values[:, :cut], values[:, cut:])


def edge_terms(head_rows, rel_rows, tail_rows, neg_rows):
    head_full = head_rows.astype(jnp.float32)
    rel_full = rel_rows.astype(jnp.float32)
    tail_full = tail_rows.astype(jnp.float32)
    head_re, head_im = split_parts(head_full)
    rel_re, rel_im = split_parts(rel_full)
    tail_re, tail_im = split_parts(tail_full)
    product = jnp.concatenate(
        [head_re * rel_re - head_im * rel_im, head_re * rel_im + head_im * rel_re], axis=1
    )
    product_low = product.astype(jnp.bfloat16)
    mirror_low = jnp.concatenate(
        [rel_re * tail_re + rel_im * tail_im, rel_re * tail_im - rel_im * tail_re], axis=1
    ).astype(jnp.bfloat16)
    positive = jnp.sum(product * tail_full, axis=1)
    inner_dims = (((1,), (1,)), ((), ()))
    tail_scores = lax.dot_general(
        product_low, neg_rows, inner_dims, preferred_element_type=jnp.float32
    )
    head_scores = lax.dot_general(
        mirror_low, neg_rows, inner_dims, preferred_element_type=jnp.float32
    )
    neg_count = neg_rows.shape[0]
    pos_grad = -jax.nn.sigmoid(-positive)
    tail_weight = (jax.nn.sigmoid(tail_scores) / neg_count).astype(jnp.bfloat16)
    head_weight = (jax.nn.sigmoid(head_scores) / neg_count).astype(jnp.bfloat16)
    product_grad = (
        jnp.dot(tail_weight, neg_rows, preferred_element_type=jnp.float32)
        + pos_grad[:, None] * tail_full
    )
    mirror_grad = jnp.dot(head_weight, neg_rows, preferred_element_type=jnp.float32)
    edge_dims = (((0,), (0,)), ((), ()))
    neg_grad = lax.dot_general(
        tail_weight, product_low, edge_dims, preferred_element_type=jnp.float32
    )
    neg_grad = neg_grad + lax.dot_general(
        head_weight, mirror_low, edge_dims, preferred_element_type=jnp.float32
    )
    grad_re, grad_im = split_parts(product_grad)
    head_grad = jnp.concatenate(
        [grad_re * rel_re + grad_im * rel_im, grad_im * rel_re - grad_re * rel_im], axis=1
    )
    back_re, back_im = split_parts(mirror_grad)
    tail_grad = pos_grad[:, None] * product + jnp.concatenate(
        [back_re * rel_re - back_im * rel_im, back_re * rel_im + back_im * rel_re], axis=1
    )
    return (head_grad, tail_grad, neg_grad)


def row_update(old_rows, old_state, gradient):
    new_state = old_state + jnp.mean(gradient * gradient, axis=1)
    new_rows = old_rows - step_rate * gradient / jnp.sqrt(new_state)[:, None]
    return (new_rows, new_state)


def shards(head_ids, rel_ids, tail_ids, neg_ids, slot_of, relations, embeddings, accumulator):
    row_count = embeddings.shape[0]
    feature_count = embeddings.shape[1]
    owner_count = lax.axis_size("ent")
    edge_count = head_ids.shape[0]
    end_ids = jnp.concatenate([head_ids, tail_ids])
    end_count = end_ids.shape[0]
    capacity = 2 * end_count // owner_count
    end_slots = slot_of[end_ids]
    owner_of = end_slots // row_count
    local_row = end_slots % row_count
    sorter = jnp.argsort(owner_of, stable=True)
    sorted_owner = owner_of[sorter]
    per_owner = jnp.sum(
        (owner_of[:, None] == jnp.arange(owner_count, dtype=jnp.int32)[None, :]).astype(jnp.int32),
        axis=0,
    )
    starting = jnp.cumsum(per_owner) - per_owner
    sorted_place = (
        sorted_owner * capacity + jnp.arange(end_count, dtype=jnp.int32) - starting[sorted_owner]
    )
    placed = jnp.zeros((end_count,), jnp.int32).at[sorter].set(sorted_place)
    requests = (
        jnp.full((owner_count * capacity,), -1, jnp.int32)
        .at[placed]
        .set(local_row)
        .reshape(owner_count, capacity)
    )
    low_table = embeddings.astype(jnp.bfloat16)
    asked_rows = lax.all_to_all(requests, "ent", split_axis=0, concat_axis=0, tiled=True)
    picked = jnp.where(
        (asked_rows >= 0)[:, :, None],
        low_table[jnp.maximum(asked_rows, 0)],
        jnp.zeros((), jnp.bfloat16),
    )
    returned = lax.all_to_all(picked, "ent", split_axis=0, concat_axis=0, tiled=True)
    fetched, asked_rows = (returned, asked_rows)
    end_rows = fetched.reshape(owner_count * capacity, feature_count)[placed]
    neg_local = slot_of[neg_ids] % row_count
    own_negs = low_table[neg_local]
    neg_rows = lax.all_gather(own_negs, "ent", axis=0, tiled=True)
    rel_rows = relations[rel_ids]
    head_grad, tail_grad, neg_grad = edge_terms(
        end_rows[:edge_count], rel_rows, end_rows[edge_count:], neg_rows
    )
    neg_part = lax.psum_scatter(neg_grad, "ent", scatter_dimension=0, tiled=True)
    outgoing = (
        jnp.zeros((owner_count * capacity, feature_count), jnp.float32)
        .at[placed]
        .set(jnp.concatenate([head_grad, tail_grad], axis=0))
    )
    incoming = lax.all_to_all(
        outgoing.reshape(owner_count, capacity, feature_count),
        "ent",
        split_axis=0,
        concat_axis=0,
        tiled=True,
    ).reshape(-1, feature_count)
    targets = jnp.where(asked_rows >= 0, asked_rows, row_count).reshape(-1)
    partial_sum = jax.ops.segment_sum(incoming, targets, num_segments=row_count + 1)[:row_count]
    partial_sum = partial_sum.at[neg_local].add(neg_part)
    summed = lax.psum(partial_sum, "rep")
    new_rows, new_state = row_update(embeddings, accumulator, summed)
    return (new_rows, new_state)


def solution(mesh):
    placed = (
        P(("ent", "rep")),
        P(("ent", "rep")),
        P(("ent", "rep")),
        P("ent"),
        P(),
        P(),
        P("ent", None),
        P("ent"),
    )
    return jax.shard_map(
        shards, mesh=mesh, in_specs=placed, out_specs=(P("ent", None), P("ent")), check_vma=False
    )
```

profile of v0, /device:TPU:0, one launch (start us, length us, event | category | flops | bytes accessed | tf_op | source)
XLA Modules:
  0.0 261.9 jit_solution(16662489668703026024)
XLA Ops:
  7.2 0.9 compare_select_fusion.2
  8.1 3.1 %gather_fusion = s32[512]{0:T(512)S(1)} fusion(s32[32768]{0:T(1024)S(1)} %copy-done, s32[1024]{0:T(1024)S(1)} %pad_clamp_fusion.5), kind=kCustom, calls=%fused_computation | custom fusion | bytes 6144 | tf_op jit(solution)/shard_map/gather | solution.py:77
  11.2 0.1 convert_reduce_fusion
  11.4 3.8 %sort.17 = (s32[512]{0:T(512)}, s32[512]{0:T(512)S(1)}) sort(s32[512]{0:T(512)S(1)} %get-tuple-element.38, s32[512]{0:T(512)S(1)} %iota.11), dimensions={0}, to_apply=%region_0.1 | sort | flops 4608 | bytes 8192 | tf_op jit(solution)/shard_map/jit(argsort)/sort | solution.py:80
  15.1 3.5 %gather_fusion.1 = s32[512]{0:T(512)S(1)} fusion(s32[512]{0:T(512)S(1)} %get-tuple-element.38, s32[1024]{0:T(1024)S(1)} %pad_clamp_fusion.4), kind=kCustom, calls=%fused_computation.1 | custom fusion | bytes 6144 | tf_op jit(solution)/shard_map/gather | solution.py:81
  18.6 0.1 copy.45
  18.8 0.1 reduce.1
  18.9 0.7 fusion.31
  19.6 4.4 %compare_select_fusion.3 = (s32[512,1]{0,1:T(1,128)S(1)}, s32[512,1]{0,1:T(1,128)S(1)}) fusion(s32[]{:T(128)} %bitcast.14, s32[]{:T(128)} %bitcast.15, s32[]{:T(128)} %bitcast.16, s32[]{:T(128)} %bitcast.17, s32[]{:T(128)} %bitcast.18, s32[]{:T(128)} %bitcast.20, s32[]{:T(128)} %bitcast.19, s32[512,1]{0,1:T(1,128)S(1)} %bitcast.53), kind=kLoop, calls=%fused_computation.63 | loop fusion | flops 7680 | bytes 6172 | tf_op jit(solution)/shard_map/gather | solution.py:88
  24.0 0.1 compare_reduce_fusion.8
  24.0 5.7 %select_subtract_fusion = s32[512]{0:T(512)S(1)} fusion(pred[512]{0:T(512)(128)(4,1)S(1)} %get-tuple-element.20, pred[512]{0:T(512)(128)(4,1)S(1)} %get-tuple-element.19, pred[512]{0:T(512)(128)(4,1)S(1)} %get-tuple-element.18, pred[512]{0:T(512)(128)(4,1)S(1)} %get-tuple-element.17, pred[512]{0:T(512)(128)(4,1)S(1)} %get-tuple-element.16, ...), kind=kLoop, calls=%fused_computation.90 | loop fusion | flops 6144 | bytes 10788 | tf_op jit(solution)/shard_map/sub | solution.py:88
  29.7 2.4 scatter_custom_fusion
  32.2 2.4 scatter_custom_fusion.1
  34.6 0.7 all_to_all.14
  35.3 8.3 %all-to-all-start = ((s32[16,1,64]{2,1,0:T(1,128)}), s32[16,1,64]{2,1,0:T(1,128)S(1)}, u32[]{:S(2)}, u32[]{:S(2)}) async-start(s32[16,1,64]{2,1,0:T(1,128)} %all_to_all.14), calls=%async_computation | async-start | bytes 16384 | tf_op jit(solution)/shard_map/all_to_all | solution.py:98
  43.7 3.4 %copy.54 = f32[2048,400]{1,0:T(8,128)} copy(f32[2048,400]{0,1:T(8,128)S(1)} %copy-done.2) | data formatting | bytes 6553600 | tf_op args[6]
  47.0 2.5 convert_element_type.26
  49.5 1.4 all-to-all-done
  50.9 0.1 reshape.293
  51.0 4.0 %gather_fusion.2 = bf16[1024,400]{1,0:T(8,128)(2,1)S(1)} fusion(bf16[2048,400]{1,0:T(8,128)(2,1)S(1)} %convert_element_type.26, s32[1024]{0:T(1024)S(1)} %broadcast_clamp_fusion), kind=kCustom, calls=%fused_computation.2 | custom fusion | bytes 1642496 | tf_op jit(solution)/shard_map/gather | solution.py:101
  55.0 1.2 broadcast_select_fusion
  56.1 5.5 %all-to-all-start.1 = ((bf16[16,64,400]{2,1,0:T(8,128)(2,1)}), bf16[16,64,400]{2,1,0:T(8,128)(2,1)S(1)}, u32[]{:S(2)}, u32[]{:S(2)}) async-start(bf16[16,64,400]{2,1,0:T(8,128)(2,1)} %broadcast_select_fusion), calls=%async_computation.1 | async-start | bytes 2097152 | tf_op jit(solution)/shard_map/all_to_all | solution.py:104
  61.7 0.7 gather_fusion.5
  62.4 0.6 gather_fusion.6
  63.0 6.0 %copy.50 = bf16[4096,400]{1,0:T(8,128)(2,1)} copy(bf16[4096,400]{0,1:T(8,128)(2,1)} %param.13) | data formatting | bytes 6553600 | tf_op args[5]
  69.0 3.9 %gather_fusion.4 = bf16[256,400]{1,0:T(8,128)(2,1)S(1)} fusion(bf16[4096,400]{1,0:T(8,128)(2,1)} %copy.50, s32[1024]{0:T(1024)S(1)} %pad_clamp_fusion.2), kind=kCustom, calls=%fused_computation.4 | custom fusion | bytes 410624 | tf_op jit(solution)/shard_map/gather | solution.py:110
  73.0 0.1 copy.51
  73.1 42.7 %all-gather = bf16[256,400]{1,0:T(8,128)(2,1)S(1)} all-gather(bf16[16,400]{1,0:T(8,128)(2,1)S(1)} %gather_fusion.6), channel_id=2, replica_groups=mesh['ent'=16,'rep'=2] {'ent'}, dimensions={0}, use_global_device_ids=true | all-gather | bytes 217600 | tf_op jit(solution)/shard_map/all_gather | solution.py:109
  115.9 2.0 gather_fusion.3
  117.9 0.1 copy.56
  118.1 0.1 copy.57
  118.3 0.1 multiply_subtract_fusion.2
  118.3 0.1 multiply_reduce_fusion.1
  118.4 0.3 fusion.10
  118.8 0.3 convolution_add_fusion.1
  119.0 0.1 multiply_add_fusion.1
  119.2 0.2 copy-done.3
  119.4 0.4 copy-done.7
  119.8 0.3 fusion.11
  120.1 0.3 fusion.32
  120.4 0.1 multiply_subtract_fusion
  120.5 0.3 copy-done.5
  120.8 0.1 maximum_add_fusion
  120.8 0.1 pad_maximum_fusion
  120.9 0.3 copy.53
  121.3 3.6 %scatter_custom_fusion.2 = f32[1024,400]{1,0:T(8,128)} fusion(s32[512]{0:T(512)S(1)} %compare_select_fusion.9, f32[512,400]{1,0:T(8,128)S(1)} %copy.53, f32[]{:T(128)} %constant.29.clone.1), kind=kCustom, calls=%fused_computation.30 | custom fusion | bytes 1638404 | tf_op jit(solution)/shard_map/scatter | solution.py:118
  125.0 3.7 %all-to-all-start.2 = ((f32[16,64,400]{2,1,0:T(8,128)}), f32[16,64,400]{2,1,0:T(8,128)S(1)}, u32[]{:S(2)}, u32[]{:S(2)}) async-start(f32[16,64,400]{2,1,0:T(8,128)} %bitcast.30), calls=%async_computation.2 | async-start | bytes 4194304 | tf_op jit(solution)/shard_map/all_to_all | solution.py:120
  128.7 0.0 reduce-scatter.2.cloned.1.call-start
  128.8 0.3 fusion.15
  129.1 1.1 convolution_add_fusion
  130.3 0.5 broadcast.384
  130.8 0.7 reduce.22
  131.5 0.1 all_to_all.16
  131.5 37.4 %all-to-all-done.2 = f32[16,64,400]{2,1,0:T(8,128)S(1)} async-done(((f32[16,64,400]{2,1,0:T(8,128)}), f32[16,64,400]{2,1,0:T(8,128)S(1)}, u32[]{:S(2)}, u32[]{:S(2)}) %all-to-all-start.2) | async-done | bytes 1638432 | tf_op jit(solution)/shard_map/all_to_all | solution.py:120
  168.9 9.2 %scatter_custom_fusion.3 = f32[2049,400]{1,0:T(8,128)} fusion(s32[1024]{0:T(1024)S(1)} %bitcast.56, f32[1024,400]{1,0:T(8,128)S(1)} %bitcast.50, f32[]{:T(128)} %constant.29.clone.1), kind=kCustom, calls=%fused_computation.14 | custom fusion | flops 409600 | bytes 3278404 | tf_op jit(solution)/shard_map/scatter-add | solution.py:128
  178.1 4.6 %slice.95 = f32[2048,400]{1,0:T(8,128)} slice(f32[2049,400]{1,0:T(8,128)} %scatter_custom_fusion.3), slice={[0:2048], [0:400]} | slice | bytes 6553600 | tf_op jit(solution)/shard_map/slice | solution.py:128
  182.7 29.2 %reduce-scatter.2.cloned.1.call-done = f32[16,400]{1,0:T(8,128)} async-done(((f32[256,400]{1,0:T(8,128)}), f32[16,400]{1,0:T(8,128)}) %reduce-scatter.2.cloned.1.call-update) | async-done | bytes 25616 | tf_op jit(solution)/shard_map/reduce_scatter | solution.py:114
  211.9 5.0 %scatter_fusion = f32[2048,400]{1,0:T(8,128)} fusion(f32[2048,400]{1,0:T(8,128)} %slice.95, s32[16]{0:T(128)S(1)} %fusion.24, f32[16,400]{1,0:T(8,128)} %reduce-scatter.2.cloned.1.call-done), kind=kCustom, calls=%fused_computation.11 | custom fusion | flops 6400 | bytes 76864 | tf_op jit(solution)/shard_map/scatter-add | solution.py:129
  217.0 24.6 %all-reduce.2.cloned.1.call-done = f32[2048,400]{1,0:T(8,128)} async-done(((f32[2048,400]{1,0:T(8,128)}), f32[2048,400]{1,0:T(8,128)}) %all-reduce.2.cloned.1.call-update) | async-done | bytes 3276816 | tf_op jit(solution)/shard_map/psum | solution.py:130
  241.6 2.7 %multiply_reduce_fusion = f32[2048]{0:T(1024)S(1)} fusion(f32[2048,400]{1,0:T(8,128)} %all-reduce.2.cloned.1.call-done), kind=kLoop, calls=%fused_computation.13 | loop fusion | flops 1636352 | bytes 3284992 | tf_op jit(solution)/shard_map/reduce_sum | solution.py:64
  244.3 0.6 fusion.29
  244.9 0.1 copy-done.1
  245.0 4.9 %divide_subtract_fusion = f32[2048,400]{1,0:T(8,128)} fusion(f32[2048,400]{1,0:T(8,128)S(1)} %copy-done.1, f32[2048,400]{1,0:T(8,128)} %all-reduce.2.cloned.1.call-done, f32[2048]{0:T(1024)S(1)} %get-tuple-element.21), kind=kLoop, calls=%fused_computation.12 | loop fusion | flops 2457600 | bytes 9838592 | tf_op jit(solution)/shard_map/sub | solution.py:65
  249.9 5.2 %copy.55 = f32[2048,400]{0,1:T(8,128)} copy(f32[2048,400]{1,0:T(8,128)} %divide_subtract_fusion) | data formatting | bytes 6553600
  (52 shorter events, 0.5 us)
Async XLA Ops:
  7.2 0.9 copy-start
  7.2 36.5 %copy-start.2 = (f32[2048,400]{0,1:T(8,128)S(1)}, f32[2048,400]{0,1:T(8,128)}, u32[]{:S(2)}) copy-start(f32[2048,400]{0,1:T(8,128)} %param.14) | copy-start | bytes 9830404
  35.3 15.6 %all-to-all-start = ((s32[16,1,64]{2,1,0:T(1,128)}), s32[16,1,64]{2,1,0:T(1,128)S(1)}, u32[]{:S(2)}, u32[]{:S(2)}) async-start(s32[16,1,64]{2,1,0:T(1,128)} %all_to_all.14), calls=%async_computation | async-start | bytes 16384 | tf_op jit(solution)/shard_map/all_to_all | solution.py:98
  54.9 6.7 %copy-start.13 = (s32[16]{0:T(128)S(1)}, s32[16]{0:T(128)}, u32[]{:S(2)}) copy-start(s32[16]{0:T(128)} %param.11) | copy-start | bytes 196
  56.1 59.8 %all-to-all-start.1 = ((bf16[16,64,400]{2,1,0:T(8,128)(2,1)}), bf16[16,64,400]{2,1,0:T(8,128)(2,1)S(1)}, u32[]{:S(2)}, u32[]{:S(2)}) async-start(bf16[16,64,400]{2,1,0:T(8,128)(2,1)} %broadcast_select_fusion), calls=%async_computation.1 | async-start | bytes 2097152 | tf_op jit(solution)/shard_map/all_to_all | solution.py:104
  61.7 7.3 %copy-start.12 = (s32[256]{0:T(256)S(1)}, s32[256]{0:T(256)}, u32[]{:S(2)}) copy-start(s32[256]{0:T(256)} %param.9) | copy-start | bytes 3076
  118.8 0.6 copy-start.3
  119.1 0.6 copy-start.7
  119.2 0.7 copy-start.9
  120.1 0.7 copy-start.5
  121.3 7.5 %copy-start.4 = (bf16[256,256]{1,0:T(8,128)(2,1)S(1)}, bf16[256,256]{1,0:T(8,128)(2,1)}, u32[]{:S(2)}) copy-start(bf16[256,256]{1,0:T(8,128)(2,1)} %copy-done.3) | copy-start | bytes 393220
  121.3 7.7 %copy-start.6 = (bf16[256,256]{1,0:T(8,128)(2,1)S(1)}, bf16[256,256]{1,0:T(8,128)(2,1)}, u32[]{:S(2)}) copy-start(bf16[256,256]{1,0:T(8,128)(2,1)} %copy-done.5) | copy-start | bytes 393220
  121.3 7.7 %copy-start.8 = (bf16[256,200]{0,1:T(8,128)(2,1)S(1)}, bf16[256,200]{0,1:T(8,128)(2,1)}, u32[]{:S(2)}) copy-start(bf16[256,200]{0,1:T(8,128)(2,1)} %copy-done.7) | copy-start | bytes 307204
  121.3 7.7 %copy-start.10 = (bf16[256,200]{0,1:T(8,128)(2,1)S(1)}, bf16[256,200]{0,1:T(8,128)(2,1)}, u32[]{:S(2)}) copy-start(bf16[256,200]{0,1:T(8,128)(2,1)} %copy-done.9) | copy-start | bytes 307204
  125.0 44.0 %all-to-all-start.2 = ((f32[16,64,400]{2,1,0:T(8,128)}), f32[16,64,400]{2,1,0:T(8,128)S(1)}, u32[]{:S(2)}, u32[]{:S(2)}) async-start(f32[16,64,400]{2,1,0:T(8,128)} %bitcast.30), calls=%async_computation.2 | async-start | bytes 4194304 | tf_op jit(solution)/shard_map/all_to_all | solution.py:120
  128.7 83.2 %reduce-scatter.2.cloned.1.call-start = ((), (), s32[]{:S(2)}) async-start(), calls=%async_computation.4 | async-start | bytes 557056 | tf_op jit(solution)/shard_map/reduce_scatter | solution.py:114
  130.2 111.3 %all-reduce.2.cloned.1.call-start = ((), (), s32[]{:S(2)}) async-start(), calls=%async_computation.5 | async-start | bytes 8388608 | tf_op jit(solution)/shard_map/psum | solution.py:130
  217.0 27.3 %copy-start.11 = (f32[2048]{0:T(1024)S(1)}, f32[2048]{0:T(1024)}, u32[]{:S(2)}) copy-start(f32[2048]{0:T(1024)} %param.15) | copy-start | bytes 24580
  241.6 3.4 %copy-start.1 = (f32[2048,400]{1,0:T(8,128)S(1)}, f32[2048,400]{1,0:T(8,128)}, u32[]{:S(2)}) copy-start(f32[2048,400]{1,0:T(8,128)} %copy.54) | copy-start | bytes 9830404
Sparse Core Ops, SparseCore 0:
  131.8 80.1 reduce-scatter.1
  217.1 24.4 all-reduce.1
where the time goes:
time: 263 us; the launch traced here: 262 us
  waiting for transfers between devices  92.6 us (35%)
  local copies, waits for them, and re-layouts  49.5 us (19%)
  blocking collectives  42.7 us (16%)
  other arithmetic  42.3 us (16%)
  starting transfers between devices  17.7 us (7%)
  between operations  14.5 us (6%)
    all_gather x1, blocking collectives, shards(): neg_rows = lax.all_gather(own_negs, 'ent', axis=0, tiled=True)  42.7 us
    all_to_all x1, waiting for transfers between devices, shards(): lax.all_to_all(outgoing.reshape(owner_count, capacity, feature_count), 'e...  37.4 us
    reduce_scatter x1, waiting for transfers between devices, shards(): lax.psum_scatter(neg_grad, 'ent', scatter_dimension=0, tiled=True)  29.2 us
    psum x1, waiting for transfers between devices, shards(): summed = lax.psum(partial_sum, 'rep')  24.6 us
    unnamed x33, local copies, waits for them, and re-layouts  16 us
    scatter-add x1, other arithmetic, shards(): jax.ops.segment_sum(incoming, targets, num_segments=row_count + 1)  9.16 us
    all_to_all x1, starting transfers between devices, shards(): lax.all_to_all(requests, 'ent', split_axis=0, concat_axis=0, tiled=True)  8.34 us
    sub x1, other arithmetic, shards(): sorted_owner * capacity + jnp.arange(end_count, dtype=jnp.int32)  5.67 us
  transfers between devices with their start and end apart: 5, of which 4 were waited for; matrix products, arithmetic and copies ran while one was open for 13% of the time, Pallas kernels for 0%

commit v1 on v0

--- a/solution.py
+++ b/solution.py
@@ -127,7 +127,7 @@
     targets = jnp.where(asked_rows >= 0, asked_rows, row_count).reshape(-1)
     partial_sum = jax.ops.segment_sum(incoming, targets, num_segments=row_count + 1)[:row_count]
     partial_sum = partial_sum.at[neg_local].add(neg_part)
-    summed = lax.psum(partial_sum, "rep")
+    summed = jnp.sum(lax.all_gather(partial_sum, "rep"), axis=0)
     new_rows, new_state = row_update(embeddings, accumulator, summed)
     return (new_rows, new_state)
 

time: 263 us -> 282 us (1.072)
  other arithmetic: 42.3 us -> 61 us
  local copies, waits for them, and re-layouts: 49.5 us -> 59.7 us
  waiting for transfers between devices: 92.6 us -> 84.2 us
    reduce_sum x0 -> x1, other arithmetic: none -> 26.1 us  [shards(): summed = jnp.sum(lax.all_gather(partial_sum, 'rep'), axis=0)]
    psum x1 -> x0, waiting for transfers between devices: 24.6 us -> none  [shards(): summed = lax.psum(partial_sum, 'rep')]
    all_gather x0 -> x1, waiting for transfers between devices: none -> 13.6 us  [shards(): summed = jnp.sum(lax.all_gather(partial_sum, 'rep'), axis=0)]
    all_gather x0 -> x1, local copies, waits for them, and re-layouts: none -> 9.39 us  [shards(): summed = jnp.sum(lax.all_gather(partial_sum, 'rep'), axis=0)]
    scatter-add x0 -> x1, local copies, waits for them, and re-layouts: none -> 5.17 us  [shards(): partial_sum = partial_sum.at[neg_local].add(neg_part)]
    unnamed x33 -> x30, local copies, waits for them, and re-layouts: 16 us -> 11.7 us
  transfers between devices with their start and end apart: 5 -> 5, of which waited for: 4 -> 4; matrix products, arithmetic and copies ran while one was open for 13% -> 11% of each run, Pallas kernels for 0% -> 0%
where the time goes in v1:
time: 282 us; the launch traced here: 281 us
  waiting for transfers between devices  84.2 us (30%)
  other arithmetic  61 us (22%)
  local copies, waits for them, and re-layouts  59.7 us (21%)
  blocking collectives  42.7 us (15%)
  starting transfers between devices  16 us (6%)
  between operations  14.5 us (5%)
    all_gather x1, blocking collectives, shards(): neg_rows = lax.all_gather(own_negs, 'ent', axis=0, tiled=True)  42.7 us
    all_to_all x1, waiting for transfers between devices, shards(): lax.all_to_all(outgoing.reshape(owner_count, capacity, feature_count), 'e...  37 us
    reduce_scatter x1, waiting for transfers between devices, shards(): lax.psum_scatter(neg_grad, 'ent', scatter_dimension=0, tiled=True)  29.5 us
    reduce_sum x1, other arithmetic, shards(): summed = jnp.sum(lax.all_gather(partial_sum, 'rep'), axis=0)  26.1 us
    all_gather x1, waiting for transfers between devices, shards(): summed = jnp.sum(lax.all_gather(partial_sum, 'rep'), axis=0)  13.6 us
    unnamed x30, local copies, waits for them, and re-layouts  11.7 us
    all_gather x1, local copies, waits for them, and re-layouts, shards(): summed = jnp.sum(lax.all_gather(partial_sum, 'rep'), axis=0)  9.39 us
    scatter-add x1, other arithmetic, shards(): jax.ops.segment_sum(incoming, targets, num_segments=row_count + 1)  9.16 us
  transfers between devices with their start and end apart: 5, of which 4 were waited for; matrix products, arithmetic and copies ran while one was open for 11% of the time, Pallas kernels for 0%

profile of v1, /device:TPU:0, one launch (start us, length us, event | category | flops | bytes accessed | tf_op | source)
XLA Modules:
  0.0 280.6 jit_solution(16003686654528126458)
XLA Ops:
  7.2 0.7 compare_select_fusion.2
  7.9 0.2 copy-done
  8.1 3.1 %gather_fusion = s32[512]{0:T(512)S(1)} fusion(s32[32768]{0:T(1024)S(1)} %copy-done, s32[1024]{0:T(1024)S(1)} %pad_clamp_fusion.5), kind=kCustom, calls=%fused_computation | custom fusion | bytes 6144 | tf_op jit(solution)/shard_map/gather | solution.py:77
  11.3 0.1 convert_reduce_fusion
  11.4 3.8 %sort.17 = (s32[512]{0:T(512)}, s32[512]{0:T(512)S(1)}) sort(s32[512]{0:T(512)S(1)} %get-tuple-element.30, s32[512]{0:T(512)S(1)} %iota.11), dimensions={0}, to_apply=%region_0.1 | sort | flops 4608 | bytes 8192 | tf_op jit(solution)/shard_map/jit(argsort)/sort | solution.py:80
  15.2 3.5 %gather_fusion.1 = s32[512]{0:T(512)S(1)} fusion(s32[512]{0:T(512)S(1)} %get-tuple-element.30, s32[1024]{0:T(1024)S(1)} %pad_clamp_fusion.4), kind=kCustom, calls=%fused_computation.1 | custom fusion | bytes 6144 | tf_op jit(solution)/shard_map/gather | solution.py:81
  18.7 0.1 copy.50
  18.8 0.1 reduce.1
  18.9 0.7 fusion.31
  19.6 4.4 %compare_select_fusion.3 = (s32[512,1]{0,1:T(1,128)S(1)}, s32[512,1]{0,1:T(1,128)S(1)}) fusion(s32[]{:T(128)} %bitcast.14, s32[]{:T(128)} %bitcast.15, s32[]{:T(128)} %bitcast.16, s32[]{:T(128)} %bitcast.17, s32[]{:T(128)} %bitcast.18, s32[]{:T(128)} %bitcast.20, s32[]{:T(128)} %bitcast.19, s32[512,1]{0,1:T(1,128)S(1)} %bitcast.55), kind=kLoop, calls=%fused_computation.63 | loop fusion | flops 7680 | bytes 6172 | tf_op jit(solution)/shard_map/gather | solution.py:88
  24.0 0.1 compare_reduce_fusion.8
  24.1 5.7 %select_subtract_fusion = s32[512]{0:T(512)S(1)} fusion(pred[512]{0:T(512)(128)(4,1)S(1)} %get-tuple-element.12, pred[512]{0:T(512)(128)(4,1)S(1)} %get-tuple-element.11, pred[512]{0:T(512)(128)(4,1)S(1)} %get-tuple-element.10, pred[512]{0:T(512)(128)(4,1)S(1)} %get-tuple-element.9, pred[512]{0:T(512)(128)(4,1)S(1)} %get-tuple-element.8, ...), kind=kLoop, calls=%fused_computation.90 | loop fusion | flops 6144 | bytes 10788 | tf_op jit(solution)/shard_map/sub | solution.py:88
  29.8 2.4 scatter_custom_fusion
  32.2 2.4 scatter_custom_fusion.1
  34.7 0.7 all_to_all.14
  35.3 8.3 %all-to-all-start = ((s32[16,1,64]{2,1,0:T(1,128)}), s32[16,1,64]{2,1,0:T(1,128)S(1)}, u32[]{:S(2)}, u32[]{:S(2)}) async-start(s32[16,1,64]{2,1,0:T(1,128)} %all_to_all.14), calls=%async_computation | async-start | bytes 16384 | tf_op jit(solution)/shard_map/all_to_all | solution.py:98
  43.7 3.1 %copy.52 = bf16[2048,400]{1,0:T(8,128)(2,1)S(1)} copy(f32[2048,400]{0,1:T(8,128)} %param.14) | data formatting | bytes 4915200 | tf_op args[6]
  46.8 4.1 %all-to-all-done = s32[16,1,64]{2,1,0:T(1,128)S(1)} async-done(((s32[16,1,64]{2,1,0:T(1,128)}), s32[16,1,64]{2,1,0:T(1,128)S(1)}, u32[]{:S(2)}, u32[]{:S(2)}) %all-to-all-start) | async-done | bytes 4128 | tf_op jit(solution)/shard_map/all_to_all | solution.py:98
  50.9 0.1 reshape.293
  51.0 4.0 %gather_fusion.2 = bf16[1024,400]{1,0:T(8,128)(2,1)S(1)} fusion(bf16[2048,400]{1,0:T(8,128)(2,1)S(1)} %copy.52, s32[1024]{0:T(1024)S(1)} %broadcast_clamp_fusion), kind=kCustom, calls=%fused_computation.2 | custom fusion | bytes 1642496 | tf_op jit(solution)/shard_map/gather | solution.py:101
  55.0 1.2 broadcast_select_fusion
  56.2 3.7 %all-to-all-start.1 = ((bf16[16,64,400]{2,1,0:T(8,128)(2,1)}), bf16[16,64,400]{2,1,0:T(8,128)(2,1)S(1)}, u32[]{:S(2)}, u32[]{:S(2)}) async-start(bf16[16,64,400]{2,1,0:T(8,128)(2,1)} %broadcast_select_fusion), calls=%async_computation.1 | async-start | bytes 2097152 | tf_op jit(solution)/shard_map/all_to_all | solution.py:104
  59.9 0.7 gather_fusion.5
  60.5 0.6 gather_fusion.6
  61.1 6.0 %copy.55 = bf16[4096,400]{1,0:T(8,128)(2,1)} copy(bf16[4096,400]{0,1:T(8,128)(2,1)} %param.13) | data formatting | bytes 6553600 | tf_op args[5]
  67.2 3.9 %gather_fusion.4 = bf16[256,400]{1,0:T(8,128)(2,1)S(1)} fusion(bf16[4096,400]{1,0:T(8,128)(2,1)} %copy.55, s32[1024]{0:T(1024)S(1)} %pad_clamp_fusion.2), kind=kCustom, calls=%fused_computation.4 | custom fusion | bytes 410624 | tf_op jit(solution)/shard_map/gather | solution.py:110
  71.1 0.1 copy.56
  71.3 42.7 %all-gather = bf16[256,400]{1,0:T(8,128)(2,1)S(1)} all-gather(bf16[16,400]{1,0:T(8,128)(2,1)S(1)} %gather_fusion.6), channel_id=2, replica_groups=mesh['ent'=16,'rep'=2] {'ent'}, dimensions={0}, use_global_device_ids=true | all-gather | bytes 217600 | tf_op jit(solution)/shard_map/all_gather | solution.py:109
  114.0 2.0 gather_fusion.3
  116.0 0.1 copy.62
  116.2 0.1 copy.63
  116.4 0.1 multiply_reduce_fusion.1
  116.6 0.3 fusion.10
  116.9 0.3 convolution_add_fusion.1
  117.2 0.1 multiply_add_fusion.1
  117.3 0.2 copy-done.2
  117.5 0.4 copy-done.6
  117.9 0.3 fusion.11
  118.3 0.3 fusion.32
  118.6 0.3 copy-done.4
  118.9 0.1 maximum_add_fusion
  119.0 0.1 pad_maximum_fusion
  119.1 0.3 copy.58
  119.4 3.6 %scatter_custom_fusion.2 = f32[1024,400]{1,0:T(8,128)} fusion(s32[512]{0:T(512)S(1)} %compare_select_fusion.9, f32[512,400]{1,0:T(8,128)S(1)} %copy.58, f32[]{:T(128)} %constant.29.clone.1), kind=kCustom, calls=%fused_computation.30 | custom fusion | bytes 1638404 | tf_op jit(solution)/shard_map/scatter | solution.py:118
  123.1 3.9 %all-to-all-start.2 = ((f32[16,64,400]{2,1,0:T(8,128)}), f32[16,64,400]{2,1,0:T(8,128)S(1)}, u32[]{:S(2)}, u32[]{:S(2)}) async-start(f32[16,64,400]{2,1,0:T(8,128)} %bitcast.30), calls=%async_computation.2 | async-start | bytes 4194304 | tf_op jit(solution)/shard_map/all_to_all | solution.py:120
  127.1 0.3 fusion.15
  127.4 1.1 convolution_add_fusion
  128.6 0.5 broadcast.384
  129.1 0.7 reduce.22
  129.8 0.1 all_to_all.16
  129.8 37.0 %all-to-all-done.2 = f32[16,64,400]{2,1,0:T(8,128)S(1)} async-done(((f32[16,64,400]{2,1,0:T(8,128)}), f32[16,64,400]{2,1,0:T(8,128)S(1)}, u32[]{:S(2)}, u32[]{:S(2)}) %all-to-all-start.2) | async-done | bytes 1638432 | tf_op jit(solution)/shard_map/all_to_all | solution.py:120
  166.9 9.2 %scatter_custom_fusion.3 = f32[2049,400]{1,0:T(8,128)} fusion(s32[1024]{0:T(1024)S(1)} %bitcast.58, f32[1024,400]{1,0:T(8,128)S(1)} %bitcast.52, f32[]{:T(128)} %constant.29.clone.1), kind=kCustom, calls=%fused_computation.14 | custom fusion | flops 409600 | bytes 3278404 | tf_op jit(solution)/shard_map/scatter-add | solution.py:128
  176.0 4.6 %slice.95 = f32[2048,400]{1,0:T(8,128)} slice(f32[2049,400]{1,0:T(8,128)} %scatter_custom_fusion.3), slice={[0:2048], [0:400]} | slice | bytes 6553600 | tf_op jit(solution)/shard_map/slice | solution.py:128
  180.6 29.5 %reduce-scatter.2.cloned.1.call-done = f32[16,400]{1,0:T(8,128)} async-done(((f32[256,400]{1,0:T(8,128)}), f32[16,400]{1,0:T(8,128)}) %reduce-scatter.2.cloned.1.call-update) | async-done | bytes 25616 | tf_op jit(solution)/shard_map/reduce_scatter | solution.py:114
  210.1 5.0 %scatter_fusion = f32[2048,400]{1,0:T(8,128)} fusion(f32[2048,400]{1,0:T(8,128)} %slice.95, s32[16]{0:T(128)S(1)} %fusion.24, f32[16,400]{1,0:T(8,128)} %reduce-scatter.2.cloned.1.call-done), kind=kCustom, calls=%fused_computation.11 | custom fusion | flops 6400 | bytes 76864 | tf_op jit(solution)/shard_map/scatter-add | solution.py:129
  215.1 5.2 %copy.59 = f32[2048,400]{0,1:T(8,128)} copy(f32[2048,400]{1,0:T(8,128)} %scatter_fusion) | data formatting | bytes 6553600 | tf_op jit(solution)/shard_map/scatter-add | solution.py:129
  220.3 13.6 %all-gather.4.cloned.1.call-done = f32[4096,400]{0,1:T(8,128)} async-done(((f32[2048,400]{0,1:T(8,128)}), f32[4096,400]{0,1:T(8,128)}) %all-gather.4.cloned.1.call-update) | async-done | bytes 6553616 | tf_op jit(solution)/shard_map/all_gather | solution.py:130
  233.9 9.4 %reshape.372 = f32[2,2048,400]{1,0,2:T(2,128)} reshape(f32[4096,400]{0,1:T(8,128)} %all-gather.4.cloned.1.call-done) | data formatting | bytes 13107200 | tf_op jit(solution)/shard_map/all_gather | solution.py:130
  243.3 26.1 %reduce_sum.38 = f32[2048,400]{0,1:T(8,128)S(1)} reduce(f32[2,2048,400]{1,0,2:T(2,128)} %reshape.372, f32[]{:T(128)} %constant.29.clone.1), dimensions={0}, to_apply=%region_10.11 | reduce | flops 819200 | bytes 9830404 | tf_op jit(solution)/shard_map/reduce_sum | solution.py:130
  269.5 0.3 multiply_reduce_fusion
  269.7 0.4 copy-done.10
  270.1 0.6 fusion.29
  270.7 0.6 copy-done.1
  271.4 2.4 divide_subtract_fusion
  (51 shorter events, 0.6 us)
Async XLA Ops:
  7.2 0.9 copy-start
  35.3 15.6 %all-to-all-start = ((s32[16,1,64]{2,1,0:T(1,128)}), s32[16,1,64]{2,1,0:T(1,128)S(1)}, u32[]{:S(2)}, u32[]{:S(2)}) async-start(s32[16,1,64]{2,1,0:T(1,128)} %all_to_all.14), calls=%async_computation | async-start | bytes 16384 | tf_op jit(solution)/shard_map/all_to_all | solution.py:98
  55.0 4.9 %copy-start.12 = (s32[16]{0:T(128)S(1)}, s32[16]{0:T(128)}, u32[]{:S(2)}) copy-start(s32[16]{0:T(128)} %param.11) | copy-start | bytes 196
  56.2 57.8 %all-to-all-start.1 = ((bf16[16,64,400]{2,1,0:T(8,128)(2,1)}), bf16[16,64,400]{2,1,0:T(8,128)(2,1)S(1)}, u32[]{:S(2)}, u32[]{:S(2)}) async-start(bf16[16,64,400]{2,1,0:T(8,128)(2,1)} %broadcast_select_fusion), calls=%async_computation.1 | async-start | bytes 2097152 | tf_op jit(solution)/shard_map/all_to_all | solution.py:104
  61.1 6.0 %copy-start.11 = (s32[256]{0:T(256)S(1)}, s32[256]{0:T(256)}, u32[]{:S(2)}) copy-start(s32[256]{0:T(256)} %param.9) | copy-start | bytes 3076
  116.9 0.6 copy-start.2
  117.3 0.6 copy-start.6
  117.3 0.7 copy-start.8
  118.2 0.7 copy-start.4
  119.4 7.6 %copy-start.3 = (bf16[256,256]{1,0:T(8,128)(2,1)S(1)}, bf16[256,256]{1,0:T(8,128)(2,1)}, u32[]{:S(2)}) copy-start(bf16[256,256]{1,0:T(8,128)(2,1)} %copy-done.2) | copy-start | bytes 393220
  119.4 7.9 %copy-start.5 = (bf16[256,256]{1,0:T(8,128)(2,1)S(1)}, bf16[256,256]{1,0:T(8,128)(2,1)}, u32[]{:S(2)}) copy-start(bf16[256,256]{1,0:T(8,128)(2,1)} %copy-done.4) | copy-start | bytes 393220
  119.4 7.9 %copy-start.7 = (bf16[256,200]{0,1:T(8,128)(2,1)S(1)}, bf16[256,200]{0,1:T(8,128)(2,1)}, u32[]{:S(2)}) copy-start(bf16[256,200]{0,1:T(8,128)(2,1)} %copy-done.6) | copy-start | bytes 307204
  119.4 7.9 %copy-start.9 = (bf16[256,200]{0,1:T(8,128)(2,1)S(1)}, bf16[256,200]{0,1:T(8,128)(2,1)}, u32[]{:S(2)}) copy-start(bf16[256,200]{0,1:T(8,128)(2,1)} %copy-done.8) | copy-start | bytes 307204
  123.1 43.8 %all-to-all-start.2 = ((f32[16,64,400]{2,1,0:T(8,128)}), f32[16,64,400]{2,1,0:T(8,128)S(1)}, u32[]{:S(2)}, u32[]{:S(2)}) async-start(f32[16,64,400]{2,1,0:T(8,128)} %bitcast.30), calls=%async_computation.2 | async-start | bytes 4194304 | tf_op jit(solution)/shard_map/all_to_all | solution.py:120
  127.0 83.1 %reduce-scatter.2.cloned.1.call-start = ((), (), s32[]{:S(2)}) async-start(), calls=%async_computation.4 | async-start | bytes 557056 | tf_op jit(solution)/shard_map/reduce_scatter | solution.py:114
  128.5 105.4 %all-gather.4.cloned.1.call-start = ((), (), s32[]{:S(2)}) async-start(), calls=%async_computation.5 | async-start | bytes 9830400 | tf_op jit(solution)/shard_map/all_gather | solution.py:130
  269.4 0.7 copy-start.10
  269.5 1.9 copy-start.1
Sparse Core Ops, SparseCore 0:
  130.1 79.9 reduce-scatter.1
  220.4 13.4 all-gather.3
